TPU v7x, 32 devices: a whole 2x2x4 slice. The times are simulated.
32 devices in a mesh: dp: 4 (over x, core), seq: 8 (over z, y).
Axes of the slice: x: 2, y: 2, z: 4, core: 2. Of those that a mesh axis runs over, the one named last changes fastest.
Arguments:
- spatial_input: bfloat16 [4, 8, 64, 256], P('dp', 'seq'), may hold values from -6 to 6
- temporal_input: bfloat16 [4, 64, 8, 256], P('dp', 'seq'), may hold values from -6 to 6
- out_cotangent: bfloat16 [4, 8, 64, 256], P('dp', 'seq'), may hold values from -6 to 6
- weights: bfloat16 [2, 256, 1024], replicated, may hold values from -3 to 3
- gains: float32 [2, 256], replicated, may hold values from 0.1 to 1.9
Outputs:
- input_grad: bfloat16 [4, 8, 64, 256], P('dp', 'seq')
- weight_grads: float32 [2, 262144], P(None, ('dp', 'seq'))
- gain_grads: float32 [2, 256], replicated
All inputs are finite; a program needn't handle non-finite values.
Results may differ from a plain program's by a relative error of at most 0.023.
Values may be sent and summed in bfloat16 or wider, within the bound.
A program may use at most 64 MiB of HBM per device.

v0:
```python
from functools import partial
import math
import jax
import jax.numpy as jnp
from jax import lax
from jax.sharding import PartitionSpec as P

HEADS = 4


def one_head(head_parts, score_scale):
    query_rows, key_rows, value_rows = head_parts
    scores = (
        jnp.einsum("gqe,gke->gqk", query_rows, key_rows, preferred_element_type=jnp.float32)
        * score_scale
    )
    probs = jax.nn.softmax(scores, axis=-1).astype(jnp.bfloat16)
    return jnp.einsum("gqk,gke->gqe", probs, value_rows, preferred_element_type=jnp.float32).astype(
        jnp.bfloat16
    )


def attend_block(block_input, gain_vector, weight, head_count):
    groups, length, model_width = block_input.shape
    head_size = model_width // head_count
    mean_sq = jnp.mean(block_input * block_input, axis=-1, keepdims=True)
    normed = (block_input * lax.rsqrt(mean_sq + 1e-06) * gain_vector).astype(jnp.bfloat16)
    w_cast = weight.astype(jnp.bfloat16)
    packed = jnp.dot(
        normed.reshape(groups * length, model_width),
        w_cast[:, : 3 * model_width],
        preferred_element_type=jnp.float32,
    ).astype(jnp.bfloat16)
    packed = jnp.transpose(
        packed.reshape(groups, length, 3, head_count, head_size), (2, 3, 0, 1, 4)
    )
    head_fn = jax.checkpoint(partial(one_head, score_scale=1.0 / math.sqrt(head_size)))
    mixed_heads = lax.map(head_fn, (packed[0], packed[1], packed[2]))
    mixed_heads = jnp.transpose(mixed_heads, (1, 2, 0, 3)).reshape(groups * length, model_width)
    result = jnp.dot(mixed_heads, w_cast[:, 3 * model_width :], preferred_element_type=jnp.float32)
    return result.reshape(groups, length, model_width)


def per_device(spatial_input, temporal_input, out_cotangent, weights, gains):
    w_float = weights.astype(jnp.float32)
    block_fn = partial(attend_block, head_count=HEADS)
    sample_count = spatial_input.shape[0] * lax.axis_size("dp")
    frame_count = spatial_input.shape[1] * lax.axis_size("seq")
    patch_count = spatial_input.shape[2]
    grad_factor = 1.0 / math.sqrt(sample_count * frame_count * patch_count)
    patch_major = jnp.swapaxes(out_cotangent[0], 0, 1)
    temporal_cot = lax.all_to_all(
        patch_major, "seq", split_axis=0, concat_axis=1, tiled=True
    ).astype(jnp.float32)
    unused_t, pullback_t = jax.vjp(
        block_fn, temporal_input[0].astype(jnp.float32), gains[1], w_float[1]
    )
    grad_ut, grad_gt, grad_wt = pullback_t(temporal_cot)
    temporal_term = (grad_wt * grad_factor).reshape(1, -1)
    mid_grad = (temporal_cot + grad_ut).astype(jnp.bfloat16)
    frame_back = lax.all_to_all(mid_grad, "seq", split_axis=1, concat_axis=0, tiled=True)
    spatial_cot = jnp.swapaxes(frame_back, 0, 1).astype(jnp.float32)
    unused_s, pullback_s = jax.vjp(
        block_fn, spatial_input[0].astype(jnp.float32), gains[0], w_float[0]
    )
    grad_us, grad_gs, grad_ws = pullback_s(spatial_cot)
    input_grad = (spatial_cot + grad_us).astype(jnp.bfloat16)[None]
    spatial_term = (grad_ws * grad_factor).reshape(1, -1)
    both_terms = jnp.concatenate([spatial_term, temporal_term], axis=0)
    grid_terms = both_terms.reshape(2, lax.axis_size("dp"), lax.axis_size("seq"), -1)
    over_frames = lax.psum_scatter(
        grid_terms.astype(jnp.bfloat16), "seq", scatter_dimension=2, tiled=True
    ).astype(jnp.float32)
    over_frames = over_frames.reshape(2, lax.axis_size("dp"), -1)
    weight_grads = (
        lax.psum_scatter(over_frames.astype(jnp.bfloat16), "dp", scatter_dimension=1, tiled=True)
        .astype(jnp.float32)
        .reshape(2, -1)
    )
    gain_grads = lax.psum(jnp.stack([grad_gs, grad_gt]) * grad_factor, ("dp", "seq"))
    return (input_grad, weight_grads, gain_grads)


def solution(mesh):
    return jax.shard_map(
        per_device,
        mesh=mesh,
        in_specs=(
            P("dp", "seq", None, None),
            P("dp", "seq", None, None),
            P("dp", "seq", None, None),
            P(),
            P(),
        ),
        out_specs=(P("dp", "seq", None, None), P(None, ("dp", "seq")), P()),
        check_vma=False,
    )
```

profile of v0, /device:TPU:0, one launch (start us, length us, event | category | flops | bytes accessed | tf_op | source)
XLA Modules:
  0.0 179.6 jit_solution(7019148246470243943)
XLA Ops:
  7.2 0.5 broadcast.288
  7.7 1.4 reduce.34
  9.1 0.6 reshape.395
  9.7 7.4 %all-to-all-start = ((bf16[8,2,1024]{2,1,0:T(2,128)(2,1)}), bf16[8,2,1024]{2,1,0:T(2,128)(2,1)S(1)}, u32[]{:S(2)}, u32[]{:S(2)}) async-start(bf16[8,2,1024]{2,1,0:T(2,128)(2,1)} %reshape.395), calls=%async_computation | async-start | bytes 65536 | tf_op jit(solution)/shard_map/all_to_all | solution.py:52
  17.3 0.7 copy-done.1
  18.1 0.6 copy-done.2
  18.9 1.3 slice_bitcast_fusion.1
  20.6 2.0 %while.59 = (s32[]{:T(128)}, bf16[4,8,8,64]{3,2,1,0:T(8,128)(2,1)S(1)}, bf16[4,8,8,64]{3,2,1,0:T(8,128)(2,1)S(1)}, bf16[4,8,8,64]{3,2,1,0:T(8,128)(2,1)S(1)}, bf16[4,8,8,64]{3,2,1,0:T(8,128)(2,1)S(1)}, /*index=5*/s32[]{:T(128)}) while((s32[]{:T(128)}, bf16[4,8,8,64]{3,2,1,0:T(8,128)(2,1)S(1)}, bf16[4,8,8,64]{3,2,1,0:T(8,128)(2,1)S(1)}, ...), condition=%wide.region_21.22_spmd, body=%wide.region_18.0_spmd.sunk | while | flops 204368 | bytes 105805 | solution.py:38
  23.1 1.6 while.58
  25.6 4.9 %while.56 = (s32[]{:T(128)}, bf16[4,8,8,64]{3,2,1,0:T(8,128)(2,1)S(1)}, bf16[4,8,8,64]{3,2,1,0:T(8,128)(2,1)S(1)}, bf16[4,8,8,64]{3,2,1,0:T(8,128)(2,1)S(1)}, bf...) while((s32[]{:T(128)}, ...), condition=%wide.region_5.6_spmd, body=%wide.region_1.5_spmd.sunk | while | flops 549215 | bytes 388997 | solution.py:38
  31.3 0.7 fusion.99
  32.0 6.0 %all-to-all-start.1 = ((bf16[8,8,256]{2,0,1:T(8,128)(2,1)}), bf16[8,8,256]{2,0,1:T(8,128)(2,1)S(1)}, u32[]{:S(2)}, u32[]{:S(2)}) async-start(bf16[8,8,256]{2,0,1:T(8,128)(2,1)} %fusion.99), calls=%async_computation.1 | async-start | bytes 65536 | tf_op jit(solution)/shard_map/all_to_all | solution.py:61
  39.3 5.4 %all-to-all-done.1 = bf16[8,8,256]{2,0,1:T(8,128)(2,1)S(1)} async-done(((bf16[8,8,256]{2,0,1:T(8,128)(2,1)}), bf16[8,8,256]{2,0,1:T(8,128)(2,1)S(1)}, u32[]{:S(2)}, u32[]{:S(2)}) %all-to-all-start.1) | async-done | bytes 32800 | tf_op jit(solution)/shard_map/all_to_all | solution.py:61
  45.0 4.7 %while.57 = (s32[]{:T(128)}, bf16[4,1,64,64]{2,3,0,1:T(8,128)(2,1)S(1)}, bf16[4,1,64,64]{2,3,0,1:T(8,128)(2,1)S(1)}, bf16[4,1,64,64]{2,3,1,0:T(8,128)(2,1)S(1)},...) while((s32[]{:T(128)}, ...), condition=%wide.region_12.13_spmd, body=%wide.region_8.12_spmd.sunk | while | flops 2727939 | bytes 431237 | solution.py:38
  51.1 1.7 pad_maximum_fusion
  52.9 0.6 copy-done.4
  53.6 0.6 dynamic-slice.2
  54.2 0.6 dynamic-slice
  55.2 0.7 fusion.117
  55.9 72.8 %all-reduce.15.cloned.1.call-done = bf16[2,4,8,8192]{3,1,0,2:T(4,128)(2,1)} async-done(((bf16[2,4,8,8192]{3,1,0,2:T(4,128)(2,1)}), bf16[2,4,8,8192]{3,1,0,2:T(4,128)(2,1)}) %all-reduce.15.cloned.1.call-update) | async-done | bytes 1048592
  128.7 1.6 dynamic-slice_bitcast_fusion.8
  130.3 0.8 copy.104
  131.1 39.6 %psum.7 = f32[2,256]{1,0:T(2,128)} all-reduce(f32[2,256]{1,0:T(2,128)S(1)} %maximum_multiply_fusion), channel_id=1, replica_groups=mesh['dp'=4,'seq'=8] {'dp','seq'}, use_global_device_ids=true, to_apply=%region_26.27 | all-reduce | flops 512 | bytes 4096 | tf_op jit(solution)/shard_map/psum | solution.py:80
  170.7 2.0 %bitcast_convert_fusion = f32[2,8192]{1,0:T(2,128)} fusion(bf16[2,4,8192]{2,0,1:T(2,128)(2,1)} %all-reduce.17.cloned.1.call-done, u32[]{:T(128)} %bitcast.79), kind=kLoop, calls=%fused_computation.171 | loop fusion | flops 16384 | bytes 98308 | tf_op jit(solution)/shard_map/reshape | solution.py:78
  (182 shorter events, 19.0 us)
Async XLA Ops:
  9.7 7.4 %copy-start = (bf16[1,8,8,256]{3,2,1,0:T(8,128)(2,1)S(1)}, bf16[1,8,8,256]{3,2,1,0:T(8,128)(2,1)}, u32[]{:S(2)}) copy-start(bf16[1,8,8,256]{3,2,1,0:T(8,128)(2,1)} %param.14) | copy-start | bytes 98308
  9.7 15.4 %all-to-all-start = ((bf16[8,2,1024]{2,1,0:T(2,128)(2,1)}), bf16[8,2,1024]{2,1,0:T(2,128)(2,1)S(1)}, u32[]{:S(2)}, u32[]{:S(2)}) async-start(bf16[8,2,1024]{2,1,0:T(2,128)(2,1)} %reshape.395), calls=%async_computation | async-start | bytes 65536 | tf_op jit(solution)/shard_map/all_to_all | solution.py:52
  17.3 0.8 copy-start.1
  18.0 0.7 copy-start.2
  32.0 12.7 %all-to-all-start.1 = ((bf16[8,8,256]{2,0,1:T(8,128)(2,1)}), bf16[8,8,256]{2,0,1:T(8,128)(2,1)S(1)}, u32[]{:S(2)}, u32[]{:S(2)}) async-start(bf16[8,8,256]{2,0,1:T(8,128)(2,1)} %fusion.99), calls=%async_computation.1 | async-start | bytes 65536 | tf_op jit(solution)/shard_map/all_to_all | solution.py:61
  38.0 90.8 %all-reduce.15.cloned.1.call-start = ((), (), s32[]{:S(2)}) async-start(), calls=%async_computation.2 | async-start | bytes 2097152
  52.9 117.9 %all-reduce.17.cloned.1.call-start = ((), (), s32[]{:S(2)}) async-start(), calls=%async_computation.3 | async-start | bytes 262144
  52.9 0.7 copy-start.4
  53.6 0.7 copy-start.3
Sparse Core Ops, SparseCore 0:
  53.0 75.6 all-reduce.14
  131.2 31.3 all-reduce.16
where the time goes:
time: 180 us
  waiting for transfers between devices  78.2 us (43%)
  blocking collectives  39.6 us (22%)
  between operations  14.4 us (8%)
  matrix products  13.7 us (8%)
  starting transfers between devices  13.5 us (8%)
  local copies, waits for them, and re-layouts  12 us (7%)
  other arithmetic  7.74 us (4%)
    unnamed x4, waiting for transfers between devices  72.8 us
    psum x1, blocking collectives, per_device(): lax.psum(jnp.stack([grad_gs, grad_gt]) * grad_factor, ('dp', 'seq'))  39.6 us
    all_to_all x1, starting transfers between devices, per_device(): lax.all_to_all(patch_major, 'seq', split_axis=0, concat_axis=1, tiled=True)  7.44 us
    all_to_all x1, starting transfers between devices, per_device(): lax.all_to_all(mid_grad, 'seq', split_axis=1, concat_axis=0, tiled=True)  5.99 us
    all_to_all x1, waiting for transfers between devices, per_device(): lax.all_to_all(mid_grad, 'seq', split_axis=1, concat_axis=0, tiled=True)  5.36 us
    dot_general x24, matrix products, one_head(): jnp.einsum('gqk,gke->gqe', probs, value_rows, preferred_element_type=jnp....  5.11 us
    dot_general x24, matrix products, one_head(): jnp.einsum('gqe,gke->gqk', query_rows, key_rows, preferred_element_type=j...  4.94 us
    unnamed x15, local copies, waits for them, and re-layouts  3.85 us
  transfers between devices with their start and end apart: 4, of which 2 were waited for; matrix products, arithmetic and copies ran while one was open for 6% of the time, Pallas kernels for 0%

commit v1 on v0

--- a/solution.py
+++ b/solution.py
@@ -77,7 +77,9 @@
         .astype(jnp.float32)
         .reshape(2, -1)
     )
-    gain_grads = lax.psum(jnp.stack([grad_gs, grad_gt]) * grad_factor, ("dp", "seq"))
+    local_array = jnp.stack([grad_gs, grad_gt]) * grad_factor
+    r2 = lax.psum(local_array, axis_name="dp")
+    gain_grads = lax.psum(r2, axis_name="seq")
     return (input_grad, weight_grads, gain_grads)
 
 

time: 180 us -> 172 us (0.956)
  blocking collectives: 39.6 us -> 26.5 us
  waiting for transfers between devices: 78.2 us -> 83.2 us
    psum x1 -> x2, blocking collectives: 39.6 us -> 26.5 us  [the longest x1 20 us: per_device(): gain_grads = lax.psum(r2, axis_name='seq')]
    unnamed x4, waiting for transfers between devices: 72.8 us -> 77.8 us
  transfers between devices with their start and end apart: 4 -> 4, of which waited for: 2 -> 3; matrix products, arithmetic and copies ran while one was open for 6% -> 6% of each run, Pallas kernels for 0% -> 0%
where the time goes in v1:
time: 172 us
  waiting for transfers between devices  83.2 us (48%)
  blocking collectives  26.5 us (15%)
  between operations  14.4 us (8%)
  matrix products  13.7 us (8%)
  starting transfers between devices  13.5 us (8%)
  local copies, waits for them, and re-layouts  12 us (7%)
  other arithmetic  7.74 us (4%)
    unnamed x4, waiting for transfers between devices  77.8 us
    psum x1, blocking collectives, per_device(): gain_grads = lax.psum(r2, axis_name='seq')  20 us
    all_to_all x1, starting transfers between devices, per_device(): lax.all_to_all(patch_major, 'seq', split_axis=0, concat_axis=1, tiled=True)  7.44 us
    psum x1, blocking collectives, per_device(): r2 = lax.psum(local_array, axis_name='dp')  6.51 us
    all_to_all x1, starting transfers between devices, per_device(): lax.all_to_all(mid_grad, 'seq', split_axis=1, concat_axis=0, tiled=True)  5.99 us
    all_to_all x1, waiting for transfers between devices, per_device(): lax.all_to_all(mid_grad, 'seq', split_axis=1, concat_axis=0, tiled=True)  5.36 us
    dot_general x24, matrix products, one_head(): jnp.einsum('gqk,gke->gqe', probs, value_rows, preferred_element_type=jnp....  5.11 us
    dot_general x24, matrix products, one_head(): jnp.einsum('gqe,gke->gqk', query_rows, key_rows, preferred_element_type=j...  4.94 us
  transfers between devices with their start and end apart: 4, of which 3 were waited for; matrix products, arithmetic and copies ran while one was open for 6% of the time, Pallas kernels for 0%

profile of v1, /device:TPU:0, one launch (start us, length us, event | category | flops | bytes accessed | tf_op | source)
XLA Modules:
  0.0 171.5 jit_solution(4637782065453445164)
XLA Ops:
  7.7 1.4 reduce.34
  9.1 0.6 reshape.395
  9.7 7.4 %all-to-all-start = ((bf16[8,2,1024]{2,1,0:T(2,128)(2,1)}), bf16[8,2,1024]{2,1,0:T(2,128)(2,1)S(1)}, u32[]{:S(2)}, u32[]{:S(2)}) async-start(bf16[8,2,1024]{2,1,0:T(2,128)(2,1)} %reshape.395), calls=%async_computation | async-start | bytes 65536 | tf_op jit(solution)/shard_map/all_to_all | solution.py:52
  17.3 0.7 copy-done.1
  18.9 1.3 slice_bitcast_fusion.1
  20.6 2.0 %while.59 = (s32[]{:T(128)}, bf16[4,8,8,64]{3,2,1,0:T(8,128)(2,1)S(1)}, bf16[4,8,8,64]{3,2,1,0:T(8,128)(2,1)S(1)}, bf16[4,8,8,64]{3,2,1,0:T(8,128)(2,1)S(1)}, bf16[4,8,8,64]{3,2,1,0:T(8,128)(2,1)S(1)}, /*index=5*/s32[]{:T(128)}) while((s32[]{:T(128)}, bf16[4,8,8,64]{3,2,1,0:T(8,128)(2,1)S(1)}, bf16[4,8,8,64]{3,2,1,0:T(8,128)(2,1)S(1)}, ...), condition=%wide.region_21.22_spmd, body=%wide.region_18.0_spmd.sunk | while | flops 204368 | bytes 105805 | solution.py:38
  23.1 1.6 while.58
  25.6 4.9 %while.56 = (s32[]{:T(128)}, bf16[4,8,8,64]{3,2,1,0:T(8,128)(2,1)S(1)}, bf16[4,8,8,64]{3,2,1,0:T(8,128)(2,1)S(1)}, bf16[4,8,8,64]{3,2,1,0:T(8,128)(2,1)S(1)}, bf...) while((s32[]{:T(128)}, ...), condition=%wide.region_5.6_spmd, body=%wide.region_1.5_spmd.sunk | while | flops 549215 | bytes 388997 | solution.py:38
  31.3 0.7 fusion.99
  32.0 6.0 %all-to-all-start.1 = ((bf16[8,8,256]{2,0,1:T(8,128)(2,1)}), bf16[8,8,256]{2,0,1:T(8,128)(2,1)S(1)}, u32[]{:S(2)}, u32[]{:S(2)}) async-start(bf16[8,8,256]{2,0,1:T(8,128)(2,1)} %fusion.99), calls=%async_computation.1 | async-start | bytes 65536 | tf_op jit(solution)/shard_map/all_to_all | solution.py:61
  39.3 5.4 %all-to-all-done.1 = bf16[8,8,256]{2,0,1:T(8,128)(2,1)S(1)} async-done(((bf16[8,8,256]{2,0,1:T(8,128)(2,1)}), bf16[8,8,256]{2,0,1:T(8,128)(2,1)S(1)}, u32[]{:S(2)}, u32[]{:S(2)}) %all-to-all-start.1) | async-done | bytes 32800 | tf_op jit(solution)/shard_map/all_to_all | solution.py:61
  45.0 4.7 %while.57 = (s32[]{:T(128)}, bf16[4,1,64,64]{2,3,0,1:T(8,128)(2,1)S(1)}, bf16[4,1,64,64]{2,3,0,1:T(8,128)(2,1)S(1)}, bf16[4,1,64,64]{2,3,1,0:T(8,128)(2,1)S(1)},...) while((s32[]{:T(128)}, ...), condition=%wide.region_12.13_spmd, body=%wide.region_8.12_spmd.sunk | while | flops 2727939 | bytes 431237 | solution.py:38
  51.1 1.7 %pad_maximum_fusion = bf16[2,4,8,8192]{3,1,0,2:T(4,128)(2,1)} fusion(bf16[1,4,8,8192]{3,1,0,2:T(4,128)(2,1)S(1)} %copy.103, bf16[1,4,8,8192]{3,1,0,2:T(4,128)(2,1)S(1)} %copy.102), kind=kLoop, calls=%fused_computation.110 | loop fusion | flops 524288 | bytes 2097152 | tf_op jit(solution)/shard_map/concatenate | solution.py:69
  52.9 0.6 copy-done.4
  53.6 0.6 dynamic-slice.2
  54.2 0.6 dynamic-slice
  55.2 0.7 fusion.117
  55.9 72.8 %all-reduce.15.cloned.1.call-done = bf16[2,4,8,8192]{3,1,0,2:T(4,128)(2,1)} async-done(((bf16[2,4,8,8192]{3,1,0,2:T(4,128)(2,1)}), bf16[2,4,8,8192]{3,1,0,2:T(4,128)(2,1)}) %all-reduce.15.cloned.1.call-update) | async-done | bytes 1048592
  128.7 1.6 dynamic-slice_bitcast_fusion.8
  130.3 0.8 copy.104
  131.1 6.5 %psum.14 = f32[2,256]{1,0:T(2,128)S(1)} all-reduce(f32[2,256]{1,0:T(2,128)S(1)} %maximum_multiply_fusion), channel_id=1, replica_groups=mesh['dp'=4,'seq'=8] {'dp'}, use_global_device_ids=true, to_apply=%region_26.27 | all-reduce | flops 512 | bytes 4096 | tf_op jit(solution)/shard_map/psum | solution.py:81
  137.6 20.0 %psum.15 = f32[2,256]{1,0:T(2,128)} all-reduce(f32[2,256]{1,0:T(2,128)S(1)} %psum.14), channel_id=1, replica_groups=mesh['dp'=4,'seq'=8] {'seq'}, use_global_device_ids=true, to_apply=%region_27.28 | all-reduce | flops 512 | bytes 4096 | tf_op jit(solution)/shard_map/psum | solution.py:82
  157.6 5.0 %all-reduce.17.cloned.1.call-done = bf16[2,4,8192]{2,0,1:T(2,128)(2,1)} async-done(((bf16[2,4,8192]{2,0,1:T(2,128)(2,1)}), bf16[2,4,8192]{2,0,1:T(2,128)(2,1)}) %all-reduce.17.cloned.1.call-update) | async-done | bytes 131088
  162.7 2.0 %bitcast_convert_fusion = f32[2,8192]{1,0:T(2,128)} fusion(bf16[2,4,8192]{2,0,1:T(2,128)(2,1)} %all-reduce.17.cloned.1.call-done, u32[]{:T(128)} %bitcast.79), kind=kLoop, calls=%fused_computation.171 | loop fusion | flops 16384 | bytes 98308 | tf_op jit(solution)/shard_map/reshape | solution.py:78
  (183 shorter events, 20.1 us)
Async XLA Ops:
  9.7 7.4 %copy-start = (bf16[1,8,8,256]{3,2,1,0:T(8,128)(2,1)S(1)}, bf16[1,8,8,256]{3,2,1,0:T(8,128)(2,1)}, u32[]{:S(2)}) copy-start(bf16[1,8,8,256]{3,2,1,0:T(8,128)(2,1)} %param.14) | copy-start | bytes 98308
  9.7 15.4 %all-to-all-start = ((bf16[8,2,1024]{2,1,0:T(2,128)(2,1)}), bf16[8,2,1024]{2,1,0:T(2,128)(2,1)S(1)}, u32[]{:S(2)}, u32[]{:S(2)}) async-start(bf16[8,2,1024]{2,1,0:T(2,128)(2,1)} %reshape.395), calls=%async_computation | async-start | bytes 65536 | tf_op jit(solution)/shard_map/all_to_all | solution.py:52
  17.3 0.8 copy-start.1
  18.0 0.7 copy-start.2
  32.0 12.7 %all-to-all-start.1 = ((bf16[8,8,256]{2,0,1:T(8,128)(2,1)}), bf16[8,8,256]{2,0,1:T(8,128)(2,1)S(1)}, u32[]{:S(2)}, u32[]{:S(2)}) async-start(bf16[8,8,256]{2,0,1:T(8,128)(2,1)} %fusion.99), calls=%async_computation.1 | async-start | bytes 65536 | tf_op jit(solution)/shard_map/all_to_all | solution.py:61
  38.0 90.8 %all-reduce.15.cloned.1.call-start = ((), (), s32[]{:S(2)}) async-start(), calls=%async_computation.2 | async-start | bytes 2097152
  52.9 109.8 %all-reduce.17.cloned.1.call-start = ((), (), s32[]{:S(2)}) async-start(), calls=%async_computation.3 | async-start | bytes 262144
  52.9 0.7 copy-start.4
  53.6 0.7 copy-start.3
Sparse Core Ops, SparseCore 0:
  53.0 75.6 all-reduce.14
  131.2 31.3 all-reduce.16
